TPU v7x, 256 devices: a whole 4x4x8 slice. The times are simulated.
256 devices in a mesh: role: 2 (over core), grp: 4 (over x), seq: 32 (over z, y).
Axes of the slice: x: 4, y: 4, z: 8, core: 2. Of those that a mesh axis runs over, the one named last changes fastest.
Arguments:
- tokens: bfloat16 [8, 2048, 2048], P(('role', 'grp'), 'seq'), may hold values from -8 to 8
- parents: int32 [8, 64], P(('role', 'grp')), may hold values from 0 to 62, as said below
- route_ids: int32 [8, 2048, 8], P(('role', 'grp'), 'seq'), may hold values from 0 to 127, all different within a row; in each aligned block of 64 rows (0 to 63, 64 to 127, ..., all dimensions but the last counted through in order) at most 6 rows name the same one
- route_gates: float32 [8, 2048, 8], P(('role', 'grp'), 'seq'), may hold values from 0.02 to 0.25
- input_gain: float32 [2048], replicated, may hold values from 0.1 to 1.9
- q_gain: float32 [128], replicated, may hold values from 0.5 to 25
- k_gain: float32 [128], replicated, may hold values from 0.5 to 25
- post_gain: float32 [2048], replicated, may hold values from 0.1 to 1.9
- w_query: bfloat16 [2048, 4096], P(None, 'seq'), may hold values from -0.125 to 0.125
- w_keyval: bfloat16 [4, 2048, 256], replicated, may hold values from -0.125 to 0.125
- w_out: bfloat16 [4096, 2048], P('seq'), may hold values from -0.09375 to 0.09375
- w_gate_up: bfloat16 [128, 2, 2048, 768], P(('grp', 'seq'), None, None, 'role'), may hold values from -0.125 to 0.125
- w_down: bfloat16 [128, 768, 2048], P(('grp', 'seq'), 'role'), may hold values from -0.21875 to 0.21875
Outputs:
- layer_out: bfloat16 [8, 2048, 2048], P(('role', 'grp'), 'seq')
Inputs may be any that keep to these rules, and one draw needn't show every extreme that they name: parents[s, 0] = 0; for a >= 1, parents[s, a] < a; the last node's parent is node 62. `route_ids`: each token names 8 different experts; among the 64 tokens of one device no expert is named more than 6 times, and in every draw some expert is named exactly 6 times by the tokens of some device.
All inputs are finite; a program needn't handle non-finite values.
Results may differ from a plain program's by a relative error of at most 0.018.
The roundings to bfloat16 on the way count: a program that leaves them out, or rounds other values in their place, can miss the bound.
Values may be sent and summed in bfloat16 or wider, within the bound.
No kernel may reach another device: no remote copies, remote signals or barrier semaphores. Data moves between devices by JAX's collectives and lax.ppermute only.
A program may use at most 128 MiB of HBM per device.

v0:
```python
import math
import jax
import jax.numpy as jnp
from jax import lax
from jax.sharding import PartitionSpec as P

NODE = 32
EPSILON = 1e-06
ROPE_BASE = 1000000.0
HIGHEST = lax.Precision.HIGHEST
MASKED = -1e30


def turned_gather(arrays, axis, dims):
    turned = [jnp.moveaxis(a, dim, 0) for a, dim in zip(arrays, dims)]
    both = jnp.concatenate([t.reshape(len(t), -1) for t in turned], axis=1)
    result, at, gathered = (lax.all_gather(both, axis, axis=0, tiled=True), 0, [])
    for t, dim in zip(turned, dims):
        slab = result[:, at : at + t[0].size].reshape(-1, *t.shape[1:])
        gathered.append(jnp.moveaxis(slab, 0, dim))
        at += t[0].size
    return tuple(gathered)


def rms_scale(values, gain):
    mean_sq = jnp.mean(values * values, axis=-1, keepdims=True)
    return values * lax.rsqrt(mean_sq + EPSILON) * gain


def ancestry(parent_row, node_count):
    node_ids = jnp.arange(node_count, dtype=jnp.int32)
    parent_hot = (parent_row[:, None] == node_ids[None, :]).astype(jnp.float32)
    reach_table = jnp.maximum(parent_hot, jnp.eye(node_count, dtype=jnp.float32))
    for repeat_index in range(node_count.bit_length()):
        reach_table = (jnp.dot(reach_table, reach_table, precision=HIGHEST) > 0.5).astype(
            jnp.float32
        )
    return reach_table


def token_positions(parent_row, length):
    reach_table = ancestry(parent_row, length // NODE)
    depth = jnp.sum(reach_table, axis=1) - 1.0
    offsets = (jnp.arange(length, dtype=jnp.int32) % NODE).astype(jnp.float32)
    return (reach_table, jnp.repeat(depth, NODE) * NODE + offsets)


def rotate(values, positions):
    half_dim = values.shape[-1] // 2
    frequency = jnp.power(
        ROPE_BASE, -2.0 * jnp.arange(half_dim, dtype=jnp.float32) / values.shape[-1]
    )
    angles = positions[:, None] * frequency[None, :]
    cosine = jnp.cos(angles)[:, None, :]
    sines = jnp.sin(angles)[:, None, :]
    first_half = values[..., :half_dim]
    second = values[..., half_dim:]
    return jnp.concatenate(
        [first_half * cosine - second * sines, second * cosine + first_half * sines], axis=-1
    )


def expert_ffn(inputs, gate_up, down_proj):
    gate_proj = jnp.dot(inputs, gate_up[0], preferred_element_type=jnp.float32)
    up_proj = jnp.dot(inputs, gate_up[1], preferred_element_type=jnp.float32)
    hidden = (jax.nn.silu(gate_proj) * up_proj).astype(jnp.bfloat16)
    return jnp.dot(hidden, down_proj, preferred_element_type=jnp.float32)


def body(
    tokens,
    parents,
    route_ids,
    route_gates,
    input_gain,
    q_gain,
    k_gain,
    post_gain,
    w_query,
    w_keyval,
    w_out,
    w_gate_up,
    w_down,
):
    seq_count = lax.axis_size("seq")
    grp_count = lax.axis_size("grp")
    tok_rows = tokens.shape[1]
    model_width = tokens.shape[2]
    head_dim = q_gain.shape[0]
    local_heads = w_query.shape[1] // head_dim
    kv_count = w_keyval.shape[0]
    heads_per_kv = local_heads * seq_count // kv_count
    length = tok_rows * seq_count
    q_width = local_heads * head_dim
    residual = tokens[0].astype(jnp.float32)
    normed = rms_scale(residual, input_gain).astype(jnp.bfloat16)
    kv_index = lax.axis_index("seq") * local_heads // heads_per_kv
    keyval_weight = lax.dynamic_index_in_dim(w_keyval, kv_index, 0, keepdims=False)
    joint_weight = jnp.concatenate([w_query, keyval_weight], axis=1)
    projected = jnp.dot(
        lax.all_gather(normed, "seq", axis=0, tiled=True),
        joint_weight,
        preferred_element_type=jnp.float32,
    ).astype(jnp.bfloat16)
    reach_table, positions = token_positions(parents[0], length)
    queries = projected[:, :q_width].astype(jnp.float32).reshape(length, local_heads, head_dim)
    q_rot = rotate(rms_scale(queries, q_gain), positions).astype(jnp.bfloat16)
    keys_in = (
        projected[:, q_width : q_width + head_dim].astype(jnp.float32).reshape(length, 1, head_dim)
    )
    k_rot = rotate(rms_scale(keys_in, k_gain), positions)[:, 0].astype(jnp.bfloat16)
    values_in = projected[:, q_width + head_dim :]
    reach_rows = jnp.repeat(reach_table, NODE, axis=0)
    block_rows = min(length, 512)
    key_pos = jnp.arange(length, dtype=jnp.int32)
    inv_scale = 1.0 / math.sqrt(head_dim)

    def attend(row_start):
        q_block = lax.dynamic_slice_in_dim(q_rot, row_start, block_rows, 0)
        scores = (
            jnp.einsum("bhd,kd->hbk", q_block, k_rot, preferred_element_type=jnp.float32)
            * inv_scale
        )
        ancestors = (
            jnp.repeat(lax.dynamic_slice_in_dim(reach_rows, row_start, block_rows, 0), NODE, axis=1)
            > 0.5
        )
        query_pos = row_start + jnp.arange(block_rows, dtype=jnp.int32)
        seen = ancestors & (key_pos[None, :] <= query_pos[:, None])
        scores = jnp.where(seen[None], scores, MASKED)
        row_max = jnp.max(scores, axis=-1, keepdims=True)
        exp_scores = jnp.exp(scores - row_max)
        probs = (exp_scores / jnp.sum(exp_scores, axis=-1, keepdims=True)).astype(jnp.bfloat16)
        mixed_out = jnp.einsum("hbk,kd->bhd", probs, values_in, preferred_element_type=jnp.float32)
        return mixed_out.astype(jnp.bfloat16).reshape(block_rows, q_width)

    starts = jnp.arange(length // block_rows, dtype=jnp.int32) * block_rows
    attended = lax.map(attend, starts).reshape(length, q_width)
    token_heads = lax.all_to_all(attended, "seq", split_axis=0, concat_axis=1, tiled=True)
    attn_out = jnp.dot(
        token_heads,
        lax.all_gather(w_out, "seq", axis=0, tiled=True),
        preferred_element_type=jnp.float32,
    )
    middle = lax.optimization_barrier((residual + attn_out).astype(jnp.bfloat16))
    middle_f = middle.astype(jnp.float32)
    post_normed = rms_scale(middle_f, post_gain).astype(jnp.bfloat16)
    expert_count = grp_count * seq_count
    topk = route_ids.shape[2]
    capacity = max(4, 3 * tok_rows * topk // (2 * expert_count))
    expert_ids = route_ids[0].reshape(-1)
    expert_hot = (expert_ids[:, None] == jnp.arange(expert_count, dtype=jnp.int32)[None, :]).astype(
        jnp.int32
    )
    earlier = jnp.cumsum(expert_hot, axis=0) - expert_hot
    slot_index = jnp.sum(earlier * expert_hot, axis=1)
    target = expert_ids * capacity + slot_index
    slot_hot = (
        target[:, None] == jnp.arange(expert_count * capacity, dtype=jnp.int32)[None, :]
    ).astype(jnp.bfloat16)
    placement = jnp.sum(slot_hot.reshape(tok_rows, topk, expert_count * capacity), axis=1)
    outgoing = lax.dot_general(
        placement, post_normed, (((0,), (0,)), ((), ())), preferred_element_type=jnp.float32
    )
    outgoing = outgoing.astype(jnp.bfloat16).reshape(expert_count, capacity, model_width)
    full_gate_up, full_down = turned_gather((w_gate_up[0], w_down[0]), "role", (2, 0))
    received = lax.all_to_all(outgoing, ("grp", "seq"), split_axis=0, concat_axis=0, tiled=True)
    flat_rows = received.reshape(-1, model_width)
    returned = lax.all_to_all(
        expert_ffn(flat_rows, full_gate_up, full_down).astype(jnp.bfloat16).reshape(received.shape),
        ("grp", "seq"),
        split_axis=0,
        concat_axis=0,
        tiled=True,
    )
    returned_flat = returned.reshape(expert_count * capacity, model_width)
    picked = jnp.take(returned_flat, target, axis=0).reshape(tok_rows, topk, model_width)
    moe_sum = jnp.sum(route_gates[0][:, :, None] * picked.astype(jnp.float32), axis=1)
    return (middle_f + moe_sum).astype(jnp.bfloat16).reshape(1, tok_rows, model_width)


def solution(mesh):
    in_specs = (
        P(("role", "grp"), "seq", None),
        P(("role", "grp"), None),
        P(("role", "grp"), "seq", None),
        P(("role", "grp"), "seq", None),
        P(),
        P(),
        P(),
        P(),
        P(None, "seq"),
        P(),
        P("seq", None),
        P(("grp", "seq"), None, None, "role"),
        P(("grp", "seq"), "role", None),
    )
    out_specs = P(("role", "grp"), "seq", None)
    return jax.shard_map(body, mesh=mesh, in_specs=in_specs, out_specs=out_specs, check_vma=False)
```

profile of v0, /device:TPU:32, one launch (start us, length us, event | category | flops | bytes accessed | tf_op | source)
XLA Modules:
  0.0 528.8 jit_solution(12781115510658289095)
XLA Ops:
  7.7 1.8 fusion.56
  10.3 1.9 copy.91
  12.2 4.5 pad_maximum_fusion
  20.7 88.1 %all-gather.4.cloned.1.call-done = bf16[2048,2048]{1,0:T(8,128)(2,1)} async-done(((bf16[64,2048]{1,0:T(8,128)(2,1)}), bf16[2048,2048]{1,0:T(8,128)(2,1)}) %all-gather.4.cloned.1.call-update) | async-done | bytes 8388624 | tf_op jit(solution)/shard_map/all_gather | solution.py:101
  108.9 6.8 %convolution_convert_fusion.2 = bf16[2048,384]{0,1:T(8,128)(2,1)S(1)} fusion(bf16[2048,2048]{1,0:T(8,128)(2,1)} %all-gather.4.cloned.1.call-done, bf16[2048,256]{1,0:T(8,128)(2,1)S(1)} %dynamic-slice_bitcast_fusion, bf16[2048,128]{1,0:T(8,128)(2,1)S(1)} %copy-done.6), kind=kOutput, calls=%fused_computation.27 | convolution fusion | flops 3225157632 | bytes 11534336 | tf_op jit(solution)/shard_map/dot_general | solution.py:100
  116.3 2.4 fusion.47
  119.4 35.4 %while.11 = (s32[]{:T(128)}, bf16[4,512,128]{2,1,0:T(8,128)(2,1)}, s32[4]{0:T(128)S(1)}, f32[2048,64]{0,1:T(8,128)S(1)}, bf16[2048,1,128]{0,2,1:T(8,128)(2,1)S(1...) while((s32[]{:T(128)}, bf16[4,512,128]{2,1,0:T(8,128)(2,1)}, ...), condition=%wide.region_7.8_spmd.clone, body=%wide.region_4.7_spmd.clone.sunk | while | flops 547454464 | bytes 18299552 | solution.py:138
  124.2 1.9 fusion.110
  126.7 1.5 fusion.112
  133.0 1.8 fusion.110
  135.6 1.5 fusion.112
  141.8 1.8 fusion.110
  150.7 1.8 fusion.110
  153.2 1.5 fusion.112
  154.8 7.6 %all-to-all-start = ((bf16[32,64,128]{2,1,0:T(8,128)(2,1)}), bf16[32,64,128]{2,1,0:T(8,128)(2,1)S(1)}, u32[]{:S(2)}, u32[]{:S(2)}) async-start(bf16[32,64,128]{2,1,0:T(8,128)(2,1)} %bitcast.8), calls=%async_computation | async-start | bytes 1048576 | tf_op jit(solution)/shard_map/all_to_all | solution.py:139
  163.8 19.8 %all-to-all-done = bf16[32,64,128]{2,1,0:T(8,128)(2,1)S(1)} async-done(((bf16[32,64,128]{2,1,0:T(8,128)(2,1)}), bf16[32,64,128]{2,1,0:T(8,128)(2,1)S(1)}, u32[]{:S(2)}, u32[]{:S(2)}) %all-to-all-start) | async-done | bytes 524320 | tf_op jit(solution)/shard_map/all_to_all | solution.py:139
  183.6 70.4 %all-gather.6.cloned.1.call-done = bf16[4096,2048]{1,0:T(8,128)(2,1)} async-done(((bf16[128,2048]{1,0:T(8,128)(2,1)}), bf16[4096,2048]{1,0:T(8,128)(2,1)}) %all-gather.6.cloned.1.call-update) | async-done | bytes 16777232 | tf_op jit(solution)/shard_map/all_gather | solution.py:142
  254.0 8.8 %fusion.21 = bf16[64,2048]{1,0:T(8,128)(2,1)S(1)} fusion(bf16[4096,2048]{1,0:T(8,128)(2,1)} %all-gather.6.cloned.1.call-done, bf16[1,64,2048]{2,1,0:T(8,128)(2,1)S(1)} %copy-done, bf16[32,64,128]{2,1,0:T(8,128)(2,1)S(1)} %all-to-all-done), kind=kOutput, calls=%fused_computation.30 | convolution fusion | flops 1074135040 | bytes 17825792 | tf_op jit(solution)/shard_map/dot_general | solution.py:140
  264.0 2.8 reshape.391
  266.8 13.0 %all-to-all-start.1 = ((bf16[128,6,2048]{2,1,0:T(8,128)(2,1)}), bf16[128,6,2048]{2,1,0:T(8,128)(2,1)}, u32[]{:S(2)}, u32[]{:S(2)}) async-start(bf16[128,6,2048]{2,1,0:T(8,128)(2,1)} %reshape.391), calls=%async_computation.1 | async-start | bytes 8388608 | tf_op jit(solution)/shard_map/all_to_all | solution.py:167
  279.8 3.1 all-gather.8.cloned.1.call-done
  282.9 5.8 %slice.62 = bf16[768,4096]{0,1:T(8,128)(2,1)} slice(bf16[768,6144]{0,1:T(8,128)(2,1)} %all-gather.8.cloned.1.call-done), slice={[0:768], [0:4096]} | slice | bytes 12582912 | tf_op jit(solution)/shard_map/slice | solution.py:19
  288.7 88.1 %all-to-all-done.1 = bf16[128,6,2048]{2,1,0:T(8,128)(2,1)} async-done(((bf16[128,6,2048]{2,1,0:T(8,128)(2,1)}), bf16[128,6,2048]{2,1,0:T(8,128)(2,1)}, u32[]{:S(2)}, u32[]{:S(2)}) %all-to-all-start.1) | async-done | bytes 3145760 | tf_op jit(solution)/shard_map/all_to_all | solution.py:167
  376.9 4.9 reshape.392
  381.7 5.9 %fusion.20 = f32[768,768]{1,0:T(8,128)} fusion(bf16[768,2048]{1,0:T(8,128)(2,1)S(1)} %reshape.392, bf16[2,2048,768]{2,1,0:T(8,128)(2,1)} %bitcast.135), kind=kOutput, calls=%fused_computation.26 | convolution fusion | flops 2415919104 | bytes 8650752 | tf_op jit(solution)/shard_map/dot_general | solution.py:64
  387.6 11.0 %convolution_convert_fusion = bf16[768,2048]{1,0:T(8,128)(2,1)} fusion(bf16[768,6144]{0,1:T(8,128)(2,1)} %all-gather.8.cloned.1.call-done, f32[768,768]{1,0:T(8,128)} %fusion.20, bf16[768,2048]{1,0:T(8,128)(2,1)S(1)} %reshape.392, bf16[2,2048,768]{2,1,0:T(8,128)(2,1)} %bitcast.136), kind=kOutput, calls=%fused_computation.20 | convolution fusion | flops 4836950016 | bytes 14942208 | tf_op jit(solution)/shard_map/dot_general | solution.py:67
  398.6 6.3 %reshape.395 = bf16[128,6,2048]{2,1,0:T(8,128)(2,1)} reshape(bf16[768,2048]{1,0:T(8,128)(2,1)} %convolution_convert_fusion) | data formatting | bytes 6291456 | tf_op jit(solution)/shard_map/reshape | solution.py:170
  404.9 7.9 %all-to-all-start.2 = ((bf16[128,6,2048]{2,1,0:T(8,128)(2,1)}), bf16[128,6,2048]{2,1,0:T(8,128)(2,1)}, u32[]{:S(2)}, u32[]{:S(2)}) async-start(bf16[128,6,2048]{2,1,0:T(8,128)(2,1)} %reshape.395), calls=%async_computation.2 | async-start | bytes 8388608 | tf_op jit(solution)/shard_map/all_to_all | solution.py:169
  413.2 96.1 %all-to-all-done.2 = bf16[128,6,2048]{2,1,0:T(8,128)(2,1)} async-done(((bf16[128,6,2048]{2,1,0:T(8,128)(2,1)}), bf16[128,6,2048]{2,1,0:T(8,128)(2,1)}, u32[]{:S(2)}, u32[]{:S(2)}) %all-to-all-start.2) | async-done | bytes 3145760 | tf_op jit(solution)/shard_map/all_to_all | solution.py:169
  509.3 4.9 reshape.396
  514.2 3.3 gather_fusion
  517.5 4.0 multiply_reduce_fusion
  (102 shorter events, 26.3 us)
Async XLA Ops:
  6.5 102.3 %all-gather.4.cloned.1.call-start = ((), (), s32[]{:S(2)}) async-start(), calls=%async_computation.3 | async-start | bytes 8650752 | tf_op jit(solution)/shard_map/all_gather | solution.py:101
  9.5 244.5 %all-gather.6.cloned.1.call-start = ((), (), s32[]{:S(2)}) async-start(), calls=%async_computation.4 | async-start | bytes 17301504 | tf_op jit(solution)/shard_map/all_gather | solution.py:142
  10.2 272.7 %all-gather.8.cloned.1.call-start = ((), (), s32[]{:S(2)}) async-start(), calls=%async_computation.5 | async-start | bytes 14155776 | tf_op jit(solution)/shard_map/all_gather | solution.py:17
  16.7 0.7 copy-start.7
  16.7 2.4 copy-start.1
  16.7 92.1 %copy-start.6 = (bf16[2048,128]{1,0:T(8,128)(2,1)S(1)}, bf16[2048,128]{1,0:T(8,128)(2,1)}, u32[]{:S(2)}) copy-start(bf16[2048,128]{1,0:T(8,128)(2,1)} %param.23) | copy-start | bytes 1572868
  20.7 95.3 %copy-start.4 = (f32[128]{0:T(128)S(1)}, f32[128]{0:T(128)}, u32[]{:S(2)}) copy-start(f32[128]{0:T(128)} %param.21) | copy-start | bytes 1540
  20.7 95.3 %copy-start.5 = (f32[128]{0:T(128)S(1)}, f32[128]{0:T(128)}, u32[]{:S(2)}) copy-start(f32[128]{0:T(128)} %param.20) | copy-start | bytes 1540
  154.8 99.2 %copy-start = (bf16[1,64,2048]{2,1,0:T(8,128)(2,1)S(1)}, bf16[1,64,2048]{2,1,0:T(8,128)(2,1)}, u32[]{:S(2)}) copy-start(bf16[1,64,2048]{2,1,0:T(8,128)(2,1)} %param.15) | copy-start | bytes 786436
  154.8 28.8 %all-to-all-start = ((bf16[32,64,128]{2,1,0:T(8,128)(2,1)}), bf16[32,64,128]{2,1,0:T(8,128)(2,1)S(1)}, u32[]{:S(2)}, u32[]{:S(2)}) async-start(bf16[32,64,128]{2,1,0:T(8,128)(2,1)} %bitcast.8), calls=%async_computation | async-start | bytes 1048576 | tf_op jit(solution)/shard_map/all_to_all | solution.py:139
  163.8 99.1 %copy-start.2 = (f32[2048]{0:T(1024)S(1)}, f32[2048]{0:T(1024)}, u32[]{:S(2)}) copy-start(f32[2048]{0:T(1024)} %param.22) | copy-start | bytes 24580
  266.8 110.1 %all-to-all-start.1 = ((bf16[128,6,2048]{2,1,0:T(8,128)(2,1)}), bf16[128,6,2048]{2,1,0:T(8,128)(2,1)}, u32[]{:S(2)}, u32[]{:S(2)}) async-start(bf16[128,6,2048]{2,1,0:T(8,128)(2,1)} %reshape.391), calls=%async_computation.1 | async-start | bytes 8388608 | tf_op jit(solution)/shard_map/all_to_all | solution.py:167
  404.9 8.2 %copy-start.3 = (f32[1,64,8]{1,2,0:T(8,128)S(1)}, f32[1,64,8]{1,2,0:T(8,128)}, u32[]{:S(2)}) copy-start(f32[1,64,8]{1,2,0:T(8,128)} %param.18) | copy-start | bytes 6148
  404.9 104.4 %all-to-all-start.2 = ((bf16[128,6,2048]{2,1,0:T(8,128)(2,1)}), bf16[128,6,2048]{2,1,0:T(8,128)(2,1)}, u32[]{:S(2)}, u32[]{:S(2)}) async-start(bf16[128,6,2048]{2,1,0:T(8,128)(2,1)} %reshape.395), calls=%async_computation.2 | async-start | bytes 8388608 | tf_op jit(solution)/shard_map/all_to_all | solution.py:169
Sparse Core Ops, SparseCore 0:
  9.9 98.8 all-gather.3
  111.4 142.4 all-gather.5
  255.8 27.0 all-gather.7
where the time goes:
time: 530 us; the launch traced here: 529 us
  waiting for transfers between devices  366 us (69%)
  matrix products  48.2 us (9%)
  local copies, waits for them, and re-layouts  42 us (8%)
  starting transfers between devices  28.5 us (5%)
  other arithmetic  22.3 us (4%)
  between operations  13.5 us (3%)
  loops' own time  7.92 us (1%)
    all_to_all x1, waiting for transfers between devices, body(): lax.all_to_all(expert_ffn(flat_rows, full_gate_up, full_down).astype(jnp....  96.1 us
    all_gather x1, waiting for transfers between devices, body(): lax.all_gather(normed, 'seq', axis=0, tiled=True)  88.1 us
    all_to_all x1, waiting for transfers between devices, body(): lax.all_to_all(outgoing, ('grp', 'seq'), split_axis=0, concat_axis=0, til...  88.1 us
    all_gather x1, waiting for transfers between devices, body(): lax.all_gather(w_out, 'seq', axis=0, tiled=True)  70.4 us
    all_to_all x1, waiting for transfers between devices, body(): lax.all_to_all(attended, 'seq', split_axis=0, concat_axis=1, tiled=True)  19.8 us
    all_to_all x1, starting transfers between devices, body(): lax.all_to_all(outgoing, ('grp', 'seq'), split_axis=0, concat_axis=0, til...  13 us
    dot_general x1, matrix products, expert_ffn(): return jnp.dot(hidden, down_proj, preferred_element_type=jnp.float32)  11 us
  transfers between devices with their start and end apart: 6, of which 6 were waited for; matrix products, arithmetic and copies ran while one was open for 13% of the time, Pallas kernels for 0%

commit v1 on v0

--- a/solution.py
+++ b/solution.py
@@ -9,6 +9,11 @@
 ROPE_BASE = 1000000.0
 HIGHEST = lax.Precision.HIGHEST
 MASKED = -1e30
+
+
+def gather_over(value, axis, d):
+    outgoing = jnp.stack([value] * lax.axis_size(axis))
+    return jnp.concatenate(lax.all_to_all(outgoing, axis, 0, 0), axis=d)
 
 
 def turned_gather(arrays, axis, dims):
@@ -98,9 +103,7 @@
     keyval_weight = lax.dynamic_index_in_dim(w_keyval, kv_index, 0, keepdims=False)
     joint_weight = jnp.concatenate([w_query, keyval_weight], axis=1)
     projected = jnp.dot(
-        lax.all_gather(normed, "seq", axis=0, tiled=True),
-        joint_weight,
-        preferred_element_type=jnp.float32,
+        gather_over(normed, "seq", 0), joint_weight, preferred_element_type=jnp.float32
     ).astype(jnp.bfloat16)
     reach_table, positions = token_positions(parents[0], length)
     queries = projected[:, :q_width].astype(jnp.float32).reshape(length, local_heads, head_dim)

time: 530 us -> 623 us (1.18)
  waiting for transfers between devices: 366 us -> 447 us
  starting transfers between devices: 28.5 us -> 37.1 us
    all_to_all x0 -> x1, waiting for transfers between devices: none -> 246 us  [gather_over(): return jnp.concatenate(lax.all_to_all(outgoing, axis, 0, 0), axis=d)]
    all_gather x1 -> x0, waiting for transfers between devices: 88.1 us -> none  [body(): lax.all_gather(normed, 'seq', axis=0, tiled=True)]
    all_gather x1, waiting for transfers between devices: 70.4 us -> 0.01 us  [body(): lax.all_gather(w_out, 'seq', axis=0, tiled=True)]
    all_to_all x0 -> x1, starting transfers between devices: none -> 11.5 us  [gather_over(): return jnp.concatenate(lax.all_to_all(outgoing, axis, 0, 0), axis=d)]
  transfers between devices with their start and end apart: 6 -> 6, of which waited for: 6 -> 4; matrix products, arithmetic and copies ran while one was open for 13% -> 12% of each run, Pallas kernels for 0% -> 0%
where the time goes in v1:
time: 623 us; the launch traced here: 622 us
  waiting for transfers between devices  447 us (72%)
  matrix products  48.3 us (8%)
  local copies, waits for them, and re-layouts  45.7 us (7%)
  starting transfers between devices  37.1 us (6%)
  other arithmetic  21.8 us (3%)
  between operations  13.8 us (2%)
  loops' own time  8.47 us (1%)
    all_to_all x1, waiting for transfers between devices, gather_over(): return jnp.concatenate(lax.all_to_all(outgoing, axis, 0, 0), axis=d)  246 us
    all_to_all x1, waiting for transfers between devices, body(): lax.all_to_all(expert_ffn(flat_rows, full_gate_up, full_down).astype(jnp....  95.6 us
    all_to_all x1, waiting for transfers between devices, body(): lax.all_to_all(outgoing, ('grp', 'seq'), split_axis=0, concat_axis=0, til...  89.4 us
    all_to_all x1, waiting for transfers between devices, body(): lax.all_to_all(attended, 'seq', split_axis=0, concat_axis=1, tiled=True)  14.6 us
  transfers between devices with their start and end apart: 6, of which 4 were waited for; matrix products, arithmetic and copies ran while one was open for 12% of the time, Pallas kernels for 0%

profile of v1, /device:TPU:32, one launch (start us, length us, event | category | flops | bytes accessed | tf_op | source)
XLA Modules:
  0.0 621.8 jit_solution(9639478033211976096)
XLA Ops:
  9.5 4.3 stack.5
  13.8 11.5 %all-to-all-start = ((bf16[32,64,2048]{2,1,0:T(8,128)(2,1)}), bf16[32,64,2048]{2,1,0:T(8,128)(2,1)}, u32[]{:S(2)}, u32[]{:S(2)}) async-start(bf16[32,64,2048]{2,1,0:T(8,128)(2,1)} %stack.5), calls=%async_computation | async-start | bytes 16777216 | tf_op jit(solution)/shard_map/all_to_all | solution.py:16
  26.3 4.6 pad_maximum_fusion
  33.6 1.3 dynamic-slice_bitcast_fusion
  34.9 246.2 %all-to-all-done = bf16[32,64,2048]{2,1,0:T(8,128)(2,1)} async-done(((bf16[32,64,2048]{2,1,0:T(8,128)(2,1)}), bf16[32,64,2048]{2,1,0:T(8,128)(2,1)}, u32[]{:S(2)}, u32[]{:S(2)}) %all-to-all-start) | async-done | bytes 8388640 | tf_op jit(solution)/shard_map/all_to_all | solution.py:16
  281.1 6.9 %convolution_convert_fusion.2 = bf16[2048,384]{0,1:T(8,128)(2,1)S(1)} fusion(bf16[2048,2048]{1,0:T(8,128)(2,1)} %bitcast.4, bf16[2048,256]{1,0:T(8,128)(2,1)S(1)} %dynamic-slice_bitcast_fusion, bf16[2048,128]{1,0:T(8,128)(2,1)S(1)} %copy-done.7), kind=kOutput, calls=%fused_computation.27 | convolution fusion | flops 3225157632 | bytes 11534336 | tf_op jit(solution)/shard_map/dot_general | solution.py:105
  288.7 2.4 fusion.51
  291.7 36.4 %while.11 = (s32[]{:T(128)}, bf16[4,512,128]{2,1,0:T(8,128)(2,1)}, s32[4]{0:T(128)S(1)}, f32[2048,64]{0,1:T(8,128)S(1)}, bf16[2048,1,128]{0,2,1:T(8,128)(2,1)S(1...) while((s32[]{:T(128)}, bf16[4,512,128]{2,1,0:T(8,128)(2,1)}, ...), condition=%wide.region_7.8_spmd.clone, body=%wide.region_4.7_spmd.clone.sunk | while | flops 547454464 | bytes 18299552 | solution.py:141
  296.8 1.8 fusion.112
  299.3 1.5 fusion.114
  305.9 1.8 fusion.112
  308.4 1.5 fusion.114
  315.0 1.8 fusion.112
  317.5 1.5 fusion.114
  324.1 1.9 fusion.112
  326.6 1.5 fusion.114
  328.2 8.2 %all-to-all-start.1 = ((bf16[32,64,128]{2,1,0:T(8,128)(2,1)}), bf16[32,64,128]{2,1,0:T(8,128)(2,1)S(1)}, u32[]{:S(2)}, u32[]{:S(2)}) async-start(bf16[32,64,128]{2,1,0:T(8,128)(2,1)} %bitcast.9), calls=%async_computation.1 | async-start | bytes 1048576 | tf_op jit(solution)/shard_map/all_to_all | solution.py:142
  337.8 14.6 %all-to-all-done.1 = bf16[32,64,128]{2,1,0:T(8,128)(2,1)S(1)} async-done(((bf16[32,64,128]{2,1,0:T(8,128)(2,1)}), bf16[32,64,128]{2,1,0:T(8,128)(2,1)S(1)}, u32[]{:S(2)}, u32[]{:S(2)}) %all-to-all-start.1) | async-done | bytes 524320 | tf_op jit(solution)/shard_map/all_to_all | solution.py:142
  352.4 8.8 %fusion.21 = bf16[64,2048]{1,0:T(8,128)(2,1)S(1)} fusion(bf16[4096,2048]{1,0:T(8,128)(2,1)} %all-gather.3.cloned.1.call-done, bf16[1,64,2048]{2,1,0:T(8,128)(2,1)S(1)} %copy-done, bf16[32,64,128]{2,1,0:T(8,128)(2,1)S(1)} %all-to-all-done.1), kind=kOutput, calls=%fused_computation.30 | convolution fusion | flops 1074135040 | bytes 17825792 | tf_op jit(solution)/shard_map/dot_general | solution.py:143
  362.5 2.9 reshape.409
  365.3 9.2 %all-to-all-start.2 = ((bf16[128,6,2048]{2,1,0:T(8,128)(2,1)}), bf16[128,6,2048]{2,1,0:T(8,128)(2,1)}, u32[]{:S(2)}, u32[]{:S(2)}) async-start(bf16[128,6,2048]{2,1,0:T(8,128)(2,1)} %reshape.409), calls=%async_computation.2 | async-start | bytes 8388608 | tf_op jit(solution)/shard_map/all_to_all | solution.py:170
  374.6 5.8 slice.62
  380.4 89.4 %all-to-all-done.2 = bf16[128,6,2048]{2,1,0:T(8,128)(2,1)} async-done(((bf16[128,6,2048]{2,1,0:T(8,128)(2,1)}), bf16[128,6,2048]{2,1,0:T(8,128)(2,1)}, u32[]{:S(2)}, u32[]{:S(2)}) %all-to-all-start.2) | async-done | bytes 3145760 | tf_op jit(solution)/shard_map/all_to_all | solution.py:170
  469.9 4.9 reshape.410
  474.7 5.9 fusion.20
  480.6 11.0 %convolution_convert_fusion = bf16[768,2048]{1,0:T(8,128)(2,1)} fusion(bf16[768,6144]{0,1:T(8,128)(2,1)} %all-gather.5.cloned.1.call-done, f32[768,768]{1,0:T(8,128)} %fusion.20, bf16[768,2048]{1,0:T(8,128)(2,1)S(1)} %reshape.410, bf16[2,2048,768]{2,1,0:T(8,128)(2,1)} %bitcast.142), kind=kOutput, calls=%fused_computation.20 | convolution fusion | flops 4836950016 | bytes 14942208 | tf_op jit(solution)/shard_map/dot_general | solution.py:72
  491.6 6.3 %reshape.413 = bf16[128,6,2048]{2,1,0:T(8,128)(2,1)} reshape(bf16[768,2048]{1,0:T(8,128)(2,1)} %convolution_convert_fusion) | data formatting | bytes 6291456 | tf_op jit(solution)/shard_map/reshape | solution.py:173
  497.9 8.1 %all-to-all-start.3 = ((bf16[128,6,2048]{2,1,0:T(8,128)(2,1)}), bf16[128,6,2048]{2,1,0:T(8,128)(2,1)}, u32[]{:S(2)}, u32[]{:S(2)}) async-start(bf16[128,6,2048]{2,1,0:T(8,128)(2,1)} %reshape.413), calls=%async_computation.3 | async-start | bytes 8388608 | tf_op jit(solution)/shard_map/all_to_all | solution.py:172
  506.4 95.6 %all-to-all-done.3 = bf16[128,6,2048]{2,1,0:T(8,128)(2,1)} async-done(((bf16[128,6,2048]{2,1,0:T(8,128)(2,1)}), bf16[128,6,2048]{2,1,0:T(8,128)(2,1)}, u32[]{:S(2)}, u32[]{:S(2)}) %all-to-all-start.3) | async-done | bytes 3145760 | tf_op jit(solution)/shard_map/all_to_all | solution.py:172
  602.0 4.9 reshape.414
  606.8 3.3 gather_fusion
  610.2 4.0 multiply_reduce_fusion
  (104 shorter events, 25.9 us)
Async XLA Ops:
  6.5 345.9 %all-gather.3.cloned.1.call-start = ((), (), s32[]{:S(2)}) async-start(), calls=%async_computation.4 | async-start | bytes 17301504 | tf_op jit(solution)/shard_map/all_gather | solution.py:145
  13.8 11.6 %copy-start.1 = (bf16[1,384,2048]{2,1,0:T(8,128)(2,1)S(1)}, bf16[1,384,2048]{2,1,0:T(8,128)(2,1)}, u32[]{:S(2)}) copy-start(bf16[1,384,2048]{2,1,0:T(8,128)(2,1)} %param.27) | copy-start | bytes 4718596
  13.8 267.3 %all-to-all-start = ((bf16[32,64,2048]{2,1,0:T(8,128)(2,1)}), bf16[32,64,2048]{2,1,0:T(8,128)(2,1)}, u32[]{:S(2)}, u32[]{:S(2)}) async-start(bf16[32,64,2048]{2,1,0:T(8,128)(2,1)} %stack.5), calls=%async_computation | async-start | bytes 16777216 | tf_op jit(solution)/shard_map/all_to_all | solution.py:16
  25.4 349.2 %all-gather.5.cloned.1.call-start = ((), (), s32[]{:S(2)}) async-start(), calls=%async_computation.5 | async-start | bytes 14155776 | tf_op jit(solution)/shard_map/all_gather | solution.py:22
  30.9 0.7 copy-start.8
  30.9 2.4 copy-start.2
  30.9 250.2 %copy-start.7 = (bf16[2048,128]{1,0:T(8,128)(2,1)S(1)}, bf16[2048,128]{1,0:T(8,128)(2,1)}, u32[]{:S(2)}) copy-start(bf16[2048,128]{1,0:T(8,128)(2,1)} %param.23) | copy-start | bytes 1572868
  281.1 7.3 %copy-start.5 = (f32[128]{0:T(128)S(1)}, f32[128]{0:T(128)}, u32[]{:S(2)}) copy-start(f32[128]{0:T(128)} %param.21) | copy-start | bytes 1540
  281.1 7.3 %copy-start.6 = (f32[128]{0:T(128)S(1)}, f32[128]{0:T(128)}, u32[]{:S(2)}) copy-start(f32[128]{0:T(128)} %param.20) | copy-start | bytes 1540
  328.2 24.3 %copy-start = (bf16[1,64,2048]{2,1,0:T(8,128)(2,1)S(1)}, bf16[1,64,2048]{2,1,0:T(8,128)(2,1)}, u32[]{:S(2)}) copy-start(bf16[1,64,2048]{2,1,0:T(8,128)(2,1)} %param.15) | copy-start | bytes 786436
  328.2 24.3 %all-to-all-start.1 = ((bf16[32,64,128]{2,1,0:T(8,128)(2,1)}), bf16[32,64,128]{2,1,0:T(8,128)(2,1)S(1)}, u32[]{:S(2)}, u32[]{:S(2)}) async-start(bf16[32,64,128]{2,1,0:T(8,128)(2,1)} %bitcast.9), calls=%async_computation.1 | async-start | bytes 1048576 | tf_op jit(solution)/shard_map/all_to_all | solution.py:142
  337.8 23.6 %copy-start.3 = (f32[2048]{0:T(1024)S(1)}, f32[2048]{0:T(1024)}, u32[]{:S(2)}) copy-start(f32[2048]{0:T(1024)} %param.22) | copy-start | bytes 24580
  365.3 104.5 %all-to-all-start.2 = ((bf16[128,6,2048]{2,1,0:T(8,128)(2,1)}), bf16[128,6,2048]{2,1,0:T(8,128)(2,1)}, u32[]{:S(2)}, u32[]{:S(2)}) async-start(bf16[128,6,2048]{2,1,0:T(8,128)(2,1)} %reshape.409), calls=%async_computation.2 | async-start | bytes 8388608 | tf_op jit(solution)/shard_map/all_to_all | solution.py:170
  497.9 8.4 %copy-start.4 = (f32[1,64,8]{1,2,0:T(8,128)S(1)}, f32[1,64,8]{1,2,0:T(8,128)}, u32[]{:S(2)}) copy-start(f32[1,64,8]{1,2,0:T(8,128)} %param.18) | copy-start | bytes 6148
  497.9 104.1 %all-to-all-start.3 = ((bf16[128,6,2048]{2,1,0:T(8,128)(2,1)}), bf16[128,6,2048]{2,1,0:T(8,128)(2,1)}, u32[]{:S(2)}, u32[]{:S(2)}) async-start(bf16[128,6,2048]{2,1,0:T(8,128)(2,1)} %reshape.413), calls=%async_computation.3 | async-start | bytes 8388608 | tf_op jit(solution)/shard_map/all_to_all | solution.py:172
Sparse Core Ops, SparseCore 0:
  9.9 296.3 all-gather.2
  308.1 26.9 all-gather.4
